TPU v7x, 32 devices: a whole 2x2x4 slice. The times are simulated.
32 devices in a mesh: row: 8 (over z, core), col: 4 (over y, x).
Axes of the slice: x: 2, y: 2, z: 4, core: 2. Of those that a mesh axis runs over, the one named last changes fastest.
Arguments:
- base_weight: bfloat16 [16384, 49152], P('row', 'col'), may hold values from -6 to 6
- left_factor: float32 [16384, 256], P('row', 'col'), may hold values from -6 to 6
- right_factor: float32 [256, 49152], P('row', 'col'), may hold values from -0.375 to 0.375
Outputs:
- merged: bfloat16 [16384, 49152], P(None, ('row', 'col'))
All inputs are finite; a program needn't handle non-finite values.
Results may differ from a plain program's by a relative error of at most 0.001.
Values may be sent and summed in bfloat16 or wider, within the bound.
A program may use at most 256 MiB of HBM per device.

v0:
```python
import functools

import jax
import jax.numpy as jnp
from jax import lax
from jax.experimental import pallas as pl
from jax.experimental.pallas import tpu as pltpu
from jax.sharding import PartitionSpec as P

CHUNKS = 8
AHEAD = 2
DELAY = 6
MESH = pl.DeviceIdType.MESH


def transport(nr, nc, base, left, right, served, left_all, right_all, mid, mid_right, *sems):
    (a_send, a_recv, b_send, b_recv, ra_send, ra_recv, rb_send, rb_recv,
     l1_send, l1_recv, l2_send, l2_recv, l3_send, l3_recv, own_sem) = sems
    ng = nr // nc
    half = nr // 2
    height = base.shape[0]
    width = base.shape[1] // nr
    depth = right.shape[0]
    rank, left_width = left.shape
    step = height // CHUNKS
    r = lax.axis_index("row")
    c = lax.axis_index("col")
    sibling = r + 1 - 2 * lax.rem(r, 2)

    def remote(src, dst, send, recv, row, col):
        return pltpu.make_async_remote_copy(
            src_ref=src, dst_ref=dst, send_sem=send, recv_sem=recv, device_id=(row, col), device_id_type=MESH
        )

    def shifted(value, by, size):
        return lax.rem(value + by + size, size)

    def across(k, dj, g, src, final, middle, rows, send, recv, act):
        j = shifted(c, dj, nc)
        here = c * ng + g == r
        at = pl.ds(pl.multiple_of(k * rows, 8), rows)
        source = src.at[at, pl.ds(pl.multiple_of((g * nc + j) * width, 128), width)]
        sem = (k, dj - 1, g)

        @pl.when(here)
        def _():
            to = final.at[pl.ds(pl.multiple_of(r * src.shape[0] + k * rows, 8), rows), :]
            act(remote(source, to, send.at[sem], recv.at[sem], r, j))

        @pl.when(jnp.logical_not(here))
        def _():
            to = middle.at[c, g, at, :]
            act(remote(source, to, send.at[sem], recv.at[sem], r, j))

    def start(copy):
        copy.start()

    def wait_send(copy):
        copy.wait_send()

    def arrived(k, ds, g, src, final, middle, rows, send, recv):
        at = pl.ds(pl.multiple_of(k * rows, 8), rows)
        s = shifted(c, -ds, nc)
        here = s * ng + g == r
        sem = (k, ds - 1, g)

        @pl.when(here)
        def _():
            to = final.at[pl.ds(pl.multiple_of(r * src.shape[0] + k * rows, 8), rows), :]
            remote(to, to, send.at[sem], recv.at[sem], r, s).wait_recv()

        @pl.when(jnp.logical_not(here))
        def _():
            to = middle.at[s, g, at, :]
            remote(to, to, send.at[sem], recv.at[sem], r, s).wait_recv()

    def along(k, ds, g, src, final, middle, rows, send, recv, own, act, act_own):
        at = pl.ds(pl.multiple_of(k * rows, 8), rows)
        s = shifted(c, -ds, nc)
        to_row = s * ng + g
        if ds == 0:
            source = src.at[at, pl.ds(pl.multiple_of((g * nc + c) * width, 128), width)]
        else:
            source = middle.at[s, g, at, :]
        to = final.at[pl.ds(pl.multiple_of(r * src.shape[0] + k * rows, 8), rows), :]

        @pl.when(to_row != r)
        def _():
            act(remote(source, to, send.at[k, ds, g], recv.at[k, r], to_row, c))

        if ds == 0:
            @pl.when(to_row == r)
            def _():
                act_own(pltpu.make_async_copy(source, to, own.at[k]))

    def received(k, dq, final, rows, total, send, recv):
        q = shifted(r, -dq, nr)
        to = final.at[pl.ds(pl.multiple_of(q * total + k * rows, 8), rows), :]
        remote(to, to, send.at[k, 0, 0], recv.at[k, q], q, c).wait_recv()

    big = (base, served, mid, step)
    small = (right, right_all, mid_right, depth)
    own_big = own_sem.at[pl.ds(0, CHUNKS)]
    own_small = own_sem.at[pl.ds(CHUNKS, 1)]

    def each_across(k, arrays, send, recv, act):
        for dj in range(1, nc):
            for g in range(ng):
                across(k, dj, g, *arrays, send, recv, act)

    def each_along(k, shifts, arrays, send, recv, own, act, act_own):
        for ds in shifts:
            for g in range(ng):
                along(k, ds, g, *arrays, send, recv, own, act, act_own)

    def block(s, q):
        return left_all.at[
            pl.ds(pl.multiple_of(s * rank, 8), rank), pl.ds(pl.multiple_of(q * left_width, 128), left_width)
        ]

    def first_left(d):
        return remote(left, block(c, r), l1_send.at[d - 1], l1_recv.at[d - 1], shifted(r, 2 * d, nr), c)

    def second_left(d, dj):
        q = shifted(r, -2 * d, nr)
        source = left if d == 0 else block(c, q)
        return remote(source, block(c, q), l2_send.at[d, dj - 1], l2_recv.at[d, dj - 1], r, shifted(c, dj, nc))

    def third_left(d, ds):
        q = shifted(r, -2 * d, nr)
        s = shifted(c, -ds, nc)
        source = left if d == 0 and ds == 0 else block(s, q)
        return remote(source, block(s, q), l3_send.at[d, ds], l3_recv.at[d, ds], sibling, c)

    def got(sems_send, sems_recv, s, q):
        remote(block(s, q), block(s, q), sems_send, sems_recv, r, shifted(c, 1, nc)).wait_recv()

    barrier = pltpu.get_barrier_semaphore()
    for dj in range(1, nc):
        pl.semaphore_signal(barrier, inc=1, device_id=(r, shifted(c, dj, nc)), device_id_type=MESH)
    for dq in range(1, nr):
        pl.semaphore_signal(barrier, inc=1, device_id=(shifted(r, dq, nr), c), device_id_type=MESH)
    pl.semaphore_wait(barrier, nc + nr - 2)

    each_across(0, big, a_send, a_recv, start)
    for d in range(1, half):
        first_left(d).start()
    each_across(0, small, ra_send, ra_recv, start)
    each_along(0, (0,), small, rb_send, rb_recv, own_small, start, start)
    own_left = pltpu.make_async_copy(left, block(c, r), own_sem.at[CHUNKS + 1])
    own_left.start()

    @pl.loop(1, AHEAD)
    def _(k):
        each_across(k, big, a_send, a_recv, start)

    plane = r // ng
    at_end = jnp.logical_or(r < ng, r >= nr - ng)

    def forward(k):
        for ds in range(nc):
            s = shifted(c, -ds, nc)
            late = jnp.logical_and(at_end, jnp.abs(s - plane) >= 2)
            turn = jnp.where(late, k - DELAY, k)

            @pl.when(jnp.logical_and(turn >= 0, turn < CHUNKS))
            def _():
                for g in range(ng):
                    if ds > 0:
                        arrived(turn, ds, g, *big, a_send, a_recv)
                    along(turn, ds, g, *big, b_send, b_recv, own_big, start, start)

    @pl.loop(0, CHUNKS + DELAY)
    def _(k):
        @pl.when(k + AHEAD < CHUNKS)
        def _():
            each_across(k + AHEAD, big, a_send, a_recv, start)

        forward(k)

        @pl.when(k == 0)
        def _():
            for g in range(ng):
                for ds in range(1, nc):
                    arrived(0, ds, g, *small, ra_send, ra_recv)
            each_along(0, range(1, nc), small, rb_send, rb_recv, own_small, start, start)

    for d in range(half):
        if d > 0:
            got(l1_send.at[d - 1], l1_recv.at[d - 1], c, shifted(r, -2 * d, nr))
        for dj in range(1, nc):
            second_left(d, dj).start()
        third_left(d, 0).start()
    for d in range(half):
        for ds in range(1, nc):
            got(l2_send.at[d, ds - 1], l2_recv.at[d, ds - 1], shifted(c, -ds, nc), shifted(r, -2 * d, nr))
            third_left(d, ds).start()
    for d in range(half):
        for ds in range(nc):
            got(l3_send.at[d, ds], l3_recv.at[d, ds], shifted(c, -ds, nc), shifted(sibling, -2 * d, nr))
            third_left(d, ds).wait_send()
        for dj in range(1, nc):
            second_left(d, dj).wait_send()
        if d > 0:
            first_left(d).wait_send()
    own_left.wait()

    def finish(copy):
        copy.wait()

    def drain(k, arrays, a, b_s, b_r, own):
        each_across(k, arrays, *a, wait_send)
        each_along(k, range(nc), arrays, b_s, b_r, own, wait_send, finish)
        for dq in range(1, nr):
            received(k, dq, arrays[1], arrays[3], arrays[0].shape[0], b_s, b_r)

    drain(0, small, (ra_send, ra_recv), rb_send, rb_recv, own_small)

    @pl.loop(0, CHUNKS)
    def _(k):
        drain(k, big, (a_send, a_recv), b_send, b_recv, own_big)


def move(base_weight, left_turned, right_factor):
    nr = lax.axis_size("row")
    nc = lax.axis_size("col")
    ng = nr // nc
    half = nr // 2
    height, stored_width = base_weight.shape
    width = stored_width // nr
    depth = right_factor.shape[0]
    rank, left_width = left_turned.shape
    out = jax.ShapeDtypeStruct
    dma = pltpu.SemaphoreType.DMA
    anywhere = pl.BlockSpec(memory_space=pl.ANY)

    def stage_sems(chunks):
        a = (chunks, nc - 1, ng)
        return [dma(a), dma(a), dma((chunks, nc, ng)), dma((chunks, nr))]

    return pl.pallas_call(
        functools.partial(transport, nr, nc),
        out_shape=[
            out((nr * height, width), base_weight.dtype),
            out((nc * rank, nr * left_width), left_turned.dtype),
            out((nr * depth, width), right_factor.dtype),
            out((nc, ng, height, width), base_weight.dtype),
            out((nc, ng, depth, width), right_factor.dtype),
        ],
        in_specs=[anywhere] * 3,
        out_specs=[anywhere] * 5,
        scratch_shapes=[
            *stage_sems(CHUNKS),
            *stage_sems(1),
            dma((half - 1,)), dma((half - 1,)),
            dma((half, nc - 1)), dma((half, nc - 1)),
            dma((half, nc)), dma((half, nc)),
            dma((CHUNKS + 2,)),
        ],
        compiler_params=pltpu.CompilerParams(collective_id=0, has_side_effects=True),
    )(base_weight, left_turned, right_factor)


def body(base_weight, left_factor, right_factor):
    served, left_all, right_all, _, _ = move(base_weight, left_factor.T, right_factor)
    delta = lax.dot_general(
        left_all, right_all, (((0,), (0,)), ((), ())),
        precision=lax.Precision.HIGH, preferred_element_type=jnp.float32,
    )
    return (served.astype(jnp.float32) + delta).astype(jnp.bfloat16)


def solution(mesh):
    placed = (P("row", "col"), P("row", "col"), P("row", "col"))
    return jax.shard_map(
        body, mesh=mesh, in_specs=placed, out_specs=P(None, ("row", "col")), check_vma=False
    )
```

profile of v0, /device:TPU:5, one launch (start us, length us, event | category | flops | bytes accessed | tf_op | source)
XLA Modules:
  0.0 1217.4 jit_solution(13730464840164307118)
XLA Ops:
  0.0 1166.0 %shard_map.37 = (bf16[16384,1536]{1,0:T(8,128)(2,1)}, f32[256,16384]{1,0:T(8,128)}, f32[256,1536]{1,0:T(8,128)}, bf16[4,2,2048,1536]{3,2,1,0:T(8,128)(2,1)}, f32[4,2,32,1536]{3,2,1,0:T(8,128)}) custom-call(bf16[2048,12288]{1,0:T(8,128)(2,1)} %base.1, f32[64,2048]{1,0:T(8,128)} %bitcast.3, f32[32,12288]{1,0:T(8,128)} %right.1), custom_call_target="tpu_custom_call" | custom-call | tf_op jit(solution)/shard_map/pallas_call | solution.py:241
  1166.0 51.4 %add_convert_fusion = bf16[16384,1536]{1,0:T(8,128)(2,1)} fusion(bf16[16384,1536]{1,0:T(8,128)(2,1)} %get-tuple-element.8, f32[256,16384]{1,0:T(8,128)} %get-tuple-element.9, f32[256,1536]{1,0:T(8,128)} %get-tuple-element.10), kind=kOutput, calls=%fused_computation | convolution fusion | flops 38730203136 | bytes 119013376 | tf_op jit(solution)/shard_map/dot_general | solution.py:266
where the time goes:
time: 1220 us
  Pallas kernels  1170 us (96%)
  matrix products  51.4 us (4%)
    pallas_call x1, Pallas kernels, move(): pl.pallas_call(functools.partial(transport, nr, nc), out_shape=[out((nr *...  1170 us
    dot_general x1, matrix products, body(): lax.dot_general(left_all, right_all, (((0,), (0,)), ((), ())), precision=...  51.4 us

commit v1 on v0

--- a/solution.py
+++ b/solution.py
@@ -7,22 +7,25 @@
 from jax.experimental.pallas import tpu as pltpu
 from jax.sharding import PartitionSpec as P
 
-CHUNKS = 8
-AHEAD = 2
-DELAY = 6
+PARTS = 16
+CHUNKS = 15
+AHEAD = 3
+DELAY = 11
 MESH = pl.DeviceIdType.MESH
 
 
-def transport(nr, nc, base, left, right, served, left_all, right_all, mid, mid_right, *sems):
+def transport(nr, nc, base, left, right, served, left_all, right_all, tail, mid, mid_right, *sems):
     (a_send, a_recv, b_send, b_recv, ra_send, ra_recv, rb_send, rb_recv,
-     l1_send, l1_recv, l2_send, l2_recv, l3_send, l3_recv, own_sem) = sems
+     l1_send, l1_recv, l2_send, l2_recv, l3_send, l3_recv, t_send, t_recv, own_sem) = sems
     ng = nr // nc
-    half = nr // 2
+    planes = nr // 2
+    near = planes // 2
     height = base.shape[0]
     width = base.shape[1] // nr
     depth = right.shape[0]
     rank, left_width = left.shape
-    step = height // CHUNKS
+    step = height // PARTS
+    late_rows = height - CHUNKS * step
     r = lax.axis_index("row")
     c = lax.axis_index("col")
     sibling = r + 1 - 2 * lax.rem(r, 2)
@@ -113,27 +116,84 @@
             for g in range(ng):
                 along(k, ds, g, *arrays, send, recv, own, act, act_own)
 
+    def late_across(dj, g, act):
+        j = shifted(c, dj, nc)
+        source = base.at[pl.ds(CHUNKS * step, late_rows), pl.ds(pl.multiple_of((g * nc + j) * width, 128), width)]
+        act(remote(source, tail.at[c * ng + g], t_send.at[dj - 1, g], t_recv.at[dj - 1, g], r, j))
+
+    def late_arrived(ds, g):
+        s = shifted(c, -ds, nc)
+        to = tail.at[s * ng + g]
+        remote(to, to, t_send.at[ds - 1, g], t_recv.at[ds - 1, g], r, s).wait_recv()
+
+    def late_own(g):
+        source = base.at[pl.ds(CHUNKS * step, late_rows), pl.ds(pl.multiple_of((g * nc + c) * width, 128), width)]
+        return pltpu.make_async_copy(source, tail.at[c * ng + g], own_sem.at[CHUNKS + 2 + g])
+
+    def each_late(act):
+        for dj in range(1, nc):
+            for g in range(ng):
+                late_across(dj, g, act)
+
     def block(s, q):
         return left_all.at[
             pl.ds(pl.multiple_of(s * rank, 8), rank), pl.ds(pl.multiple_of(q * left_width, 128), left_width)
         ]
 
-    def first_left(d):
-        return remote(left, block(c, r), l1_send.at[d - 1], l1_recv.at[d - 1], shifted(r, 2 * d, nr), c)
+    place = r // 2
+    core = lax.rem(r, 2)
+    first = place // near * near
+
+    def beside(e):
+        return first + lax.rem(place - first + e + near, near)
+
+    def over(p):
+        return shifted(p, near, planes)
+
+    def held(m):
+        p = beside(-(m % near))
+        return (p if m < near else over(p)) * 2 + core
+
+    def first_left(m):
+        to = beside(m) if m < near else over(place)
+        return remote(left, block(c, r), l1_send.at[m - 1], l1_recv.at[m - 1], to * 2 + core, c)
+
+    def passed_left(m):
+        q = held(near)
+        return remote(block(c, q), block(c, q), l1_send.at[near + m - 1], l1_recv.at[near + m - 1], beside(m) * 2 + core, c)
 
     def second_left(d, dj):
-        q = shifted(r, -2 * d, nr)
+        q = held(d)
         source = left if d == 0 else block(c, q)
         return remote(source, block(c, q), l2_send.at[d, dj - 1], l2_recv.at[d, dj - 1], r, shifted(c, dj, nc))
 
     def third_left(d, ds):
-        q = shifted(r, -2 * d, nr)
+        q = held(d)
         s = shifted(c, -ds, nc)
         source = left if d == 0 and ds == 0 else block(s, q)
         return remote(source, block(s, q), l3_send.at[d, ds], l3_recv.at[d, ds], sibling, c)
 
     def got(sems_send, sems_recv, s, q):
         remote(block(s, q), block(s, q), sems_send, sems_recv, r, shifted(c, 1, nc)).wait_recv()
+
+    def pass_left():
+        got(l1_send.at[near - 1], l1_recv.at[near - 1], c, held(near))
+        for m in range(1, near):
+            passed_left(m).start()
+
+    def spread_left():
+        for d in range(planes):
+            if d > 0 and d != near:
+                got(l1_send.at[d - 1], l1_recv.at[d - 1], c, held(d))
+            for dj in range(1, nc):
+                second_left(d, dj).start()
+            third_left(d, 0).start()
+
+    def share_left():
+        for d in range(planes):
+            for ds in range(1, nc):
+                got(l2_send.at[d, ds - 1], l2_recv.at[d, ds - 1], shifted(c, -ds, nc), held(d))
+                third_left(d, ds).start()
 
     barrier = pltpu.get_barrier_semaphore()
     for dj in range(1, nc):
@@ -143,8 +203,8 @@
     pl.semaphore_wait(barrier, nc + nr - 2)
 
     each_across(0, big, a_send, a_recv, start)
-    for d in range(1, half):
-        first_left(d).start()
+    for m in range(near, 0, -1):
+        first_left(m).start()
     each_across(0, small, ra_send, ra_recv, start)
     each_along(0, (0,), small, rb_send, rb_recv, own_small, start, start)
     own_left = pltpu.make_async_copy(left, block(c, r), own_sem.at[CHUNKS + 1])
@@ -176,7 +236,16 @@
         def _():
             each_across(k + AHEAD, big, a_send, a_recv, start)
 
+        @pl.when(k + AHEAD == CHUNKS)
+        def _():
+            each_late(start)
+            for g in range(ng):
+                late_own(g).start()
+
         forward(k)
+
+        for at, act in ((1, pass_left), (5, spread_left), (9, share_left)):
+            pl.when(k == at)(act)
 
         @pl.when(k == 0)
         def _():
@@ -185,24 +254,16 @@
                     arrived(0, ds, g, *small, ra_send, ra_recv)
             each_along(0, range(1, nc), small, rb_send, rb_recv, own_small, start, start)
 
-    for d in range(half):
-        if d > 0:
-            got(l1_send.at[d - 1], l1_recv.at[d - 1], c, shifted(r, -2 * d, nr))
-        for dj in range(1, nc):
-            second_left(d, dj).start()
-        third_left(d, 0).start()
-    for d in range(half):
-        for ds in range(1, nc):
-            got(l2_send.at[d, ds - 1], l2_recv.at[d, ds - 1], shifted(c, -ds, nc), shifted(r, -2 * d, nr))
-            third_left(d, ds).start()
-    for d in range(half):
+    for d in range(planes):
         for ds in range(nc):
-            got(l3_send.at[d, ds], l3_recv.at[d, ds], shifted(c, -ds, nc), shifted(sibling, -2 * d, nr))
+            got(l3_send.at[d, ds], l3_recv.at[d, ds], shifted(c, -ds, nc), held(d) + sibling - r)
             third_left(d, ds).wait_send()
         for dj in range(1, nc):
             second_left(d, dj).wait_send()
-        if d > 0:
-            first_left(d).wait_send()
+    for m in range(1, near + 1):
+        first_left(m).wait_send()
+    for m in range(1, near):
+        passed_left(m).wait_send()
     own_left.wait()
 
     def finish(copy):
@@ -214,6 +275,11 @@
         for dq in range(1, nr):
             received(k, dq, arrays[1], arrays[3], arrays[0].shape[0], b_s, b_r)
 
+    each_late(wait_send)
+    for g in range(ng):
+        late_own(g).wait()
+        for ds in range(1, nc):
+            late_arrived(ds, g)
     drain(0, small, (ra_send, ra_recv), rb_send, rb_recv, own_small)
 
     @pl.loop(0, CHUNKS)
@@ -225,11 +291,13 @@
     nr = lax.axis_size("row")
     nc = lax.axis_size("col")
     ng = nr // nc
-    half = nr // 2
+    planes = nr // 2
     height, stored_width = base_weight.shape
     width = stored_width // nr
     depth = right_factor.shape[0]
     rank, left_width = left_turned.shape
+    main_rows = height // PARTS * CHUNKS
+    late_rows = height - main_rows
     out = jax.ShapeDtypeStruct
     dma = pltpu.SemaphoreType.DMA
     anywhere = pl.BlockSpec(memory_space=pl.ANY)
@@ -244,30 +312,42 @@
             out((nr * height, width), base_weight.dtype),
             out((nc * rank, nr * left_width), left_turned.dtype),
             out((nr * depth, width), right_factor.dtype),
-            out((nc, ng, height, width), base_weight.dtype),
+            out((nr, late_rows, width), base_weight.dtype),
+            out((nc, ng, main_rows, width), base_weight.dtype),
             out((nc, ng, depth, width), right_factor.dtype),
         ],
         in_specs=[anywhere] * 3,
-        out_specs=[anywhere] * 5,
+        out_specs=[anywhere] * 6,
         scratch_shapes=[
             *stage_sems(CHUNKS),
             *stage_sems(1),
-            dma((half - 1,)), dma((half - 1,)),
-            dma((half, nc - 1)), dma((half, nc - 1)),
-            dma((half, nc)), dma((half, nc)),
-            dma((CHUNKS + 2,)),
+            dma((planes - 1,)), dma((planes - 1,)),
+            dma((planes, nc - 1)), dma((planes, nc - 1)),
+            dma((planes, nc)), dma((planes, nc)),
+            dma((nc - 1, ng)), dma((nc - 1, ng)),
+            dma((CHUNKS + 2 + ng,)),
         ],
         compiler_params=pltpu.CompilerParams(collective_id=0, has_side_effects=True),
     )(base_weight, left_turned, right_factor)
 
 
+def product(left, right):
+    return lax.dot_general(
+        left, right, (((0,), (0,)), ((), ())), precision=lax.Precision.HIGH, preferred_element_type=jnp.float32
+    )
+
+
 def body(base_weight, left_factor, right_factor):
-    served, left_all, right_all, _, _ = move(base_weight, left_factor.T, right_factor)
-    delta = lax.dot_general(
-        left_all, right_all, (((0,), (0,)), ((), ())),
-        precision=lax.Precision.HIGH, preferred_element_type=jnp.float32,
-    )
-    return (served.astype(jnp.float32) + delta).astype(jnp.bfloat16)
+    nr = lax.axis_size("row")
+    height = base_weight.shape[0]
+    served, left_all, right_all, tail, _, _ = move(base_weight, left_factor.T, right_factor)
+    late = lax.all_to_all(tail, "row", 0, 0)
+    late_rows, width = late.shape[1:]
+    merged = (served.astype(jnp.float32) + product(left_all, right_all)).astype(jnp.bfloat16)
+    late_left = jnp.concatenate([left_all[:, (q + 1) * height - late_rows:(q + 1) * height] for q in range(nr)], axis=1)
+    late_merged = late.astype(jnp.float32) + product(late_left, right_all).reshape(late.shape)
+    merged = merged.reshape(nr, height, width).at[:, height - late_rows:].set(late_merged.astype(jnp.bfloat16))
+    return merged.reshape(nr * height, width)
 
 
 def solution(mesh):

time: 1220 us -> 1230 us (level)
  Pallas kernels: 1170 us -> 1140 us
    pallas_call x1, Pallas kernels: 1170 us -> 1140 us  [move(): pl.pallas_call(functools.partial(transport, nr, nc), out_shape=[out((nr *...]
    dot_general x1 -> x2, matrix products: 51.4 us -> 57.3 us  [product(): lax.dot_general(left, right, (((0,), (0,)), ((), ())), precision=lax.Prec...]
  transfers between devices with their start and end apart: 0 -> 1, of which waited for: 0 -> 1; matrix products, arithmetic and copies ran while one was open for 0% -> 5% of each run, Pallas kernels for 0% -> 0%
where the time goes in v1:
time: 1230 us
  Pallas kernels  1140 us (93%)
  matrix products  57.3 us (5%)
    pallas_call x1, Pallas kernels, move(): pl.pallas_call(functools.partial(transport, nr, nc), out_shape=[out((nr *...  1140 us
    dot_general x2, matrix products, product(): lax.dot_general(left, right, (((0,), (0,)), ((), ())), precision=lax.Prec...  57.3 us
  transfers between devices with their start and end apart: 1, of which 1 were waited for; matrix products, arithmetic and copies ran while one was open for 5% of the time, Pallas kernels for 0%

profile of v1, /device:TPU:5, one launch (start us, length us, event | category | flops | bytes accessed | tf_op | source)
XLA Modules:
  0.0 1226.1 jit_solution(2760553827873489379)
XLA Ops:
  0.0 1139.6 %shard_map.37 = (bf16[16384,1536]{1,0:T(8,128)(2,1)}, f32[256,16384]{1,0:T(8,128)}, f32[256,1536]{1,0:T(8,128)}, bf16[8,128,1536]{2,1,0:T(8,128)(2,1)}, bf16[4,2...) custom-call(bf16[2048,12288]{1,0:T(8,128)(2,1)} %base.1, f32[64,2048]{1,0:T(8,128)} %bitcast.10, f32[32,12288]{1,0:T(8,128)} %right.1), custom_call_target="tpu_custom_call" | custom-call | tf_op jit(solution)/shard_map/pallas_call | solution.py:309
  1139.6 10.5 all-to-all-start
  1150.1 0.0 copy-start
  1150.1 1.0 slice_dynamic-update-slice_fusion.7
  1151.1 0.9 slice_dynamic-update-slice_fusion.6
  1152.1 0.9 slice_dynamic-update-slice_fusion.5
  1153.0 0.9 slice_dynamic-update-slice_fusion.4
  1153.9 0.9 slice_dynamic-update-slice_fusion.3
  1154.8 0.9 slice_dynamic-update-slice_fusion.2
  1155.7 0.9 slice_dynamic-update-slice_fusion.1
  1156.7 0.9 slice_dynamic-update-slice_fusion
  1157.6 6.0 fusion.1
  1163.6 0.0 copy-done
  1163.6 51.2 %add_convert_fusion = bf16[16384,1536]{1,0:T(8,128)(2,1)} fusion(bf16[16384,1536]{1,0:T(8,128)(2,1)} %get-tuple-element.21, f32[256,16384]{1,0:T(8,128)} %get-tuple-element.22, f32[256,1536]{1,0:T(8,128)S(1)} %copy-done), kind=kOutput, calls=%fused_computation | convolution fusion | flops 38730203136 | bytes 119013376 | tf_op jit(solution)/shard_map/dot_general | solution.py:335
  1214.8 5.8 all-to-all-done
  1220.6 5.5 fusion
Async XLA Ops:
  1139.6 81.0 %all-to-all-start = ((bf16[8,128,1536]{2,1,0:T(8,128)(2,1)}), bf16[8,128,1536]{2,1,0:T(8,128)(2,1)S(1)}, u32[]{:S(2)}, u32[]{:S(2)}) async-start(bf16[8,128,1536]{2,1,0:T(8,128)(2,1)} %get-tuple-element.24), calls=%async_computation | async-start | bytes 6291456 | tf_op jit(solution)/shard_map/all_to_all | solution.py:344
  1150.1 13.5 %copy-start = (f32[256,1536]{1,0:T(8,128)S(1)}, f32[256,1536]{1,0:T(8,128)}, u32[]{:S(2)}) copy-start(f32[256,1536]{1,0:T(8,128)} %get-tuple-element.23) | copy-start | bytes 4718596

commit v2 on v1

--- a/solution.py
+++ b/solution.py
@@ -9,8 +9,7 @@
 
 PARTS = 16
 CHUNKS = 15
-AHEAD = 3
-DELAY = 11
+AHEAD = 4
 MESH = pl.DeviceIdType.MESH
 
 
@@ -214,23 +213,14 @@
     def _(k):
         each_across(k, big, a_send, a_recv, start)
 
-    plane = r // ng
-    at_end = jnp.logical_or(r < ng, r >= nr - ng)
-
     def forward(k):
         for ds in range(nc):
-            s = shifted(c, -ds, nc)
-            late = jnp.logical_and(at_end, jnp.abs(s - plane) >= 2)
-            turn = jnp.where(late, k - DELAY, k)
-
-            @pl.when(jnp.logical_and(turn >= 0, turn < CHUNKS))
-            def _():
-                for g in range(ng):
-                    if ds > 0:
-                        arrived(turn, ds, g, *big, a_send, a_recv)
-                    along(turn, ds, g, *big, b_send, b_recv, own_big, start, start)
-
-    @pl.loop(0, CHUNKS + DELAY)
+            for g in range(ng):
+                if ds > 0:
+                    arrived(k, ds, g, *big, a_send, a_recv)
+                along(k, ds, g, *big, b_send, b_recv, own_big, start, start)
+
+    @pl.loop(0, CHUNKS)
     def _(k):
         @pl.when(k + AHEAD < CHUNKS)
         def _():

time: 1230 us -> 1160 us (0.943)
  Pallas kernels: 1140 us -> 1080 us
    pallas_call x1, Pallas kernels: 1140 us -> 1080 us  [move(): pl.pallas_call(functools.partial(transport, nr, nc), out_shape=[out((nr *...]
  transfers between devices with their start and end apart: 1 -> 1, of which waited for: 1 -> 1; matrix products, arithmetic and copies ran while one was open for 5% -> 6% of each run, Pallas kernels for 0% -> 0%
where the time goes in v2:
time: 1160 us
  Pallas kernels  1080 us (93%)
  matrix products  57.3 us (5%)
    pallas_call x1, Pallas kernels, move(): pl.pallas_call(functools.partial(transport, nr, nc), out_shape=[out((nr *...  1080 us
    dot_general x2, matrix products, product(): lax.dot_general(left, right, (((0,), (0,)), ((), ())), precision=lax.Prec...  57.3 us
  transfers between devices with their start and end apart: 1, of which 1 were waited for; matrix products, arithmetic and copies ran while one was open for 6% of the time, Pallas kernels for 0%

profile of v2, /device:TPU:5, one launch (start us, length us, event | category | flops | bytes accessed | tf_op | source)
XLA Modules:
  0.0 1157.8 jit_solution(15358187928752334563)
XLA Ops:
  0.0 1078.2 %shard_map.37 = (bf16[16384,1536]{1,0:T(8,128)(2,1)}, f32[256,16384]{1,0:T(8,128)}, f32[256,1536]{1,0:T(8,128)}, bf16[8,128,1536]{2,1,0:T(8,128)(2,1)}, bf16[4,2...) custom-call(bf16[2048,12288]{1,0:T(8,128)(2,1)} %base.1, f32[64,2048]{1,0:T(8,128)} %bitcast.10, f32[32,12288]{1,0:T(8,128)} %right.1), custom_call_target="tpu_custom_call" | custom-call | tf_op jit(solution)/shard_map/pallas_call | solution.py:299
  1078.2 3.6 all-to-all-start
  1081.8 0.0 copy-start
  1081.9 1.0 slice_dynamic-update-slice_fusion.7
  1082.9 0.9 slice_dynamic-update-slice_fusion.6
  1083.8 0.9 slice_dynamic-update-slice_fusion.5
  1084.7 0.9 slice_dynamic-update-slice_fusion.4
  1085.7 0.9 slice_dynamic-update-slice_fusion.3
  1086.6 0.9 slice_dynamic-update-slice_fusion.2
  1087.5 0.9 slice_dynamic-update-slice_fusion.1
  1088.4 0.9 slice_dynamic-update-slice_fusion
  1089.3 6.0 fusion.1
  1095.4 0.0 copy-done
  1095.4 51.2 %add_convert_fusion = bf16[16384,1536]{1,0:T(8,128)(2,1)} fusion(bf16[16384,1536]{1,0:T(8,128)(2,1)} %get-tuple-element.21, f32[256,16384]{1,0:T(8,128)} %get-tuple-element.22, f32[256,1536]{1,0:T(8,128)S(1)} %copy-done), kind=kOutput, calls=%fused_computation | convolution fusion | flops 38730203136 | bytes 119013376 | tf_op jit(solution)/shard_map/dot_general | solution.py:325
  1146.6 5.8 all-to-all-done
  1152.4 5.5 fusion
Async XLA Ops:
  1078.2 74.2 %all-to-all-start = ((bf16[8,128,1536]{2,1,0:T(8,128)(2,1)}), bf16[8,128,1536]{2,1,0:T(8,128)(2,1)S(1)}, u32[]{:S(2)}, u32[]{:S(2)}) async-start(bf16[8,128,1536]{2,1,0:T(8,128)(2,1)} %get-tuple-element.24), calls=%async_computation | async-start | bytes 6291456 | tf_op jit(solution)/shard_map/all_to_all | solution.py:334
  1081.8 13.5 %copy-start = (f32[256,1536]{1,0:T(8,128)S(1)}, f32[256,1536]{1,0:T(8,128)}, u32[]{:S(2)}) copy-start(f32[256,1536]{1,0:T(8,128)} %get-tuple-element.23) | copy-start | bytes 4718596

commit v3 on v2

--- a/solution.py
+++ b/solution.py
@@ -9,20 +9,73 @@
 
 PARTS = 16
 CHUNKS = 15
+FINE = 8
 AHEAD = 4
+CODE_AT = 1
+PASS_AT = 3
+SMALL_AT = 6
+SPREAD_AT = 7
+SHARE_AT = 13
 MESH = pl.DeviceIdType.MESH
-
-
-def transport(nr, nc, base, left, right, served, left_all, right_all, tail, mid, mid_right, *sems):
-    (a_send, a_recv, b_send, b_recv, ra_send, ra_recv, rb_send, rb_recv,
-     l1_send, l1_recv, l2_send, l2_recv, l3_send, l3_recv, t_send, t_recv, own_sem) = sems
+LANES = 128
+GROUP = 16
+OCTAVES = 251
+LOWEST = -125.0
+LEVELS = OCTAVES * 128.0 - 1.0
+
+
+def coded(value):
+    top = jnp.max(jnp.abs(value), axis=1, keepdims=True)
+    scale = jnp.maximum(top * 1.01, 1e-30).astype(jnp.bfloat16)
+    level = jnp.floor(jnp.abs(value) * (LEVELS / scale.astype(jnp.float32)) + 0.5)
+    octave = jnp.floor(level * (1.0 / 128.0))
+    word = (level * (1.0 / 128.0) - octave + 1.0) * jnp.exp2(octave + LOWEST)
+    return jnp.where(value < 0.0, -word, word).astype(jnp.bfloat16), scale
+
+
+def decoded(word, scale):
+    word = word.astype(jnp.float32)
+    size = jnp.abs(word)
+    octave = jnp.floor(jnp.log2(size))
+    level = jnp.floor((octave - LOWEST + (size * jnp.exp2(-octave) - 1.0)) * 128.0 + 0.5)
+    value = level * (scale.astype(jnp.float32) * (1.0 / LEVELS))
+    return jnp.where(word < 0.0, -value, value)
+
+
+def encode_rows(source, target, width):
+    @pl.loop(0, source.shape[0] // GROUP)
+    def _(i):
+        rows = pl.ds(pl.multiple_of(i * GROUP, GROUP), GROUP)
+        for b in range(source.shape[1] // width):
+            word, scale = coded(source[rows, b * width:(b + 1) * width])
+            target[b, rows, :width] = word
+            target[b, rows, width:] = jnp.broadcast_to(scale, (GROUP, LANES))
+
+
+def decode_rows(source, target):
+    width = target.shape[1]
+
+    @pl.loop(0, source.shape[0] // GROUP)
+    def _(i):
+        rows = pl.ds(pl.multiple_of(i * GROUP, GROUP), GROUP)
+        target[rows, :] = decoded(source[rows, :width], source[rows, width:width + 1])
+
+
+def transport(
+    nr, nc, base, left, right, served, left_all, right_all, tail, mid, mid_right,
+    left_code, left_codes, right_code, right_codes, *scratch,
+):
+    (a_send, a_recv, b_send, b_recv, fa_send, fa_recv, fb_send, fb_recv, ra_send, ra_recv, rb_send, rb_recv,
+     l1_send, l1_recv, l2_send, l2_recv, l3_send, l3_recv, t_send, t_recv, own_sem, code_sem,
+     left_in, left_out, right_in, right_out, left_words, left_values, right_words, right_values) = scratch
     ng = nr // nc
     planes = nr // 2
     near = planes // 2
     height = base.shape[0]
     width = base.shape[1] // nr
     depth = right.shape[0]
-    rank, left_width = left.shape
+    rank = left.shape[0]
+    left_width = left_code.shape[2]
     step = height // PARTS
     late_rows = height - CHUNKS * step
     r = lax.axis_index("row")
@@ -37,16 +90,24 @@
     def shifted(value, by, size):
         return lax.rem(value + by + size, size)
 
+    def piece(src, at, b):
+        if len(src.shape) == 3:
+            return src.at[b]
+        return src.at[at, pl.ds(pl.multiple_of(b * width, 128), width)]
+
+    def tall(src):
+        return src.shape[-2]
+
     def across(k, dj, g, src, final, middle, rows, send, recv, act):
         j = shifted(c, dj, nc)
         here = c * ng + g == r
         at = pl.ds(pl.multiple_of(k * rows, 8), rows)
-        source = src.at[at, pl.ds(pl.multiple_of((g * nc + j) * width, 128), width)]
+        source = piece(src, at, g * nc + j)
         sem = (k, dj - 1, g)
 
         @pl.when(here)
         def _():
-            to = final.at[pl.ds(pl.multiple_of(r * src.shape[0] + k * rows, 8), rows), :]
+            to = final.at[pl.ds(pl.multiple_of(r * tall(src) + k * rows, 8), rows), :]
             act(remote(source, to, send.at[sem], recv.at[sem], r, j))
 
         @pl.when(jnp.logical_not(here))
@@ -68,7 +129,7 @@
 
         @pl.when(here)
         def _():
-            to = final.at[pl.ds(pl.multiple_of(r * src.shape[0] + k * rows, 8), rows), :]
+            to = final.at[pl.ds(pl.multiple_of(r * tall(src) + k * rows, 8), rows), :]
             remote(to, to, send.at[sem], recv.at[sem], r, s).wait_recv()
 
         @pl.when(jnp.logical_not(here))
@@ -81,10 +142,10 @@
         s = shifted(c, -ds, nc)
         to_row = s * ng + g
         if ds == 0:
-            source = src.at[at, pl.ds(pl.multiple_of((g * nc + c) * width, 128), width)]
+            source = piece(src, at, g * nc + c)
         else:
             source = middle.at[s, g, at, :]
-        to = final.at[pl.ds(pl.multiple_of(r * src.shape[0] + k * rows, 8), rows), :]
+        to = final.at[pl.ds(pl.multiple_of(r * tall(src) + k * rows, 8), rows), :]
 
         @pl.when(to_row != r)
         def _():
@@ -101,12 +162,15 @@
         remote(to, to, send.at[k, 0, 0], recv.at[k, q], q, c).wait_recv()
 
     big = (base, served, mid, step)
-    small = (right, right_all, mid_right, depth)
+    fine = (base, served, mid, step // FINE)
+    small = (right_code, right_codes, mid_right, depth)
+    order = (nc // 2, *(d for d in range(1, nc) if d != nc // 2))
     own_big = own_sem.at[pl.ds(0, CHUNKS)]
     own_small = own_sem.at[pl.ds(CHUNKS, 1)]
+    own_fine = own_sem.at[pl.ds(CHUNKS + 2 + ng, FINE)]
 
     def each_across(k, arrays, send, recv, act):
-        for dj in range(1, nc):
+        for dj in order:
             for g in range(ng):
                 across(k, dj, g, *arrays, send, recv, act)
 
@@ -135,7 +199,7 @@
                 late_across(dj, g, act)
 
     def block(s, q):
-        return left_all.at[
+        return left_codes.at[
             pl.ds(pl.multiple_of(s * rank, 8), rank), pl.ds(pl.multiple_of(q * left_width, 128), left_width)
         ]
 
@@ -155,7 +219,7 @@
 
     def first_left(m):
         to = beside(m) if m < near else over(place)
-        return remote(left, block(c, r), l1_send.at[m - 1], l1_recv.at[m - 1], to * 2 + core, c)
+        return remote(left_code.at[0], block(c, r), l1_send.at[m - 1], l1_recv.at[m - 1], to * 2 + core, c)
 
     def passed_left(m):
         q = held(near)
@@ -163,13 +227,13 @@
 
     def second_left(d, dj):
         q = held(d)
-        source = left if d == 0 else block(c, q)
+        source = left_code.at[0] if d == 0 else block(c, q)
         return remote(source, block(c, q), l2_send.at[d, dj - 1], l2_recv.at[d, dj - 1], r, shifted(c, dj, nc))
 
     def third_left(d, ds):
         q = held(d)
         s = shifted(c, -ds, nc)
-        source = left if d == 0 and ds == 0 else block(s, q)
+        source = left_code.at[0] if d == 0 and ds == 0 else block(s, q)
         return remote(source, block(s, q), l3_send.at[d, ds], l3_recv.at[d, ds], sibling, c)
 
     def got(sems_send, sems_recv, s, q):
@@ -201,26 +265,48 @@
         pl.semaphore_signal(barrier, inc=1, device_id=(shifted(r, dq, nr), c), device_id_type=MESH)
     pl.semaphore_wait(barrier, nc + nr - 2)
 
-    each_across(0, big, a_send, a_recv, start)
-    for m in range(near, 0, -1):
-        first_left(m).start()
-    each_across(0, small, ra_send, ra_recv, start)
-    each_along(0, (0,), small, rb_send, rb_recv, own_small, start, start)
-    own_left = pltpu.make_async_copy(left, block(c, r), own_sem.at[CHUNKS + 1])
-    own_left.start()
-
-    @pl.loop(1, AHEAD)
+    fetch_left = pltpu.make_async_copy(left, left_in, code_sem.at[0])
+    fetch_right = pltpu.make_async_copy(right, right_in, code_sem.at[1])
+    fetch_left.start()
+    fetch_right.start()
+    for k in range(FINE):
+        each_across(k, fine, fa_send, fa_recv, start)
+        each_along(k, (0,), fine, fb_send, fb_recv, own_fine, start, start)
+
+    @pl.loop(1, AHEAD + 1)
     def _(k):
         each_across(k, big, a_send, a_recv, start)
 
-    def forward(k):
-        for ds in range(nc):
-            for g in range(ng):
-                if ds > 0:
-                    arrived(k, ds, g, *big, a_send, a_recv)
-                along(k, ds, g, *big, b_send, b_recv, own_big, start, start)
-
-    @pl.loop(0, CHUNKS)
+    own_left = pltpu.make_async_copy(left_code.at[0], block(c, r), own_sem.at[CHUNKS + 1])
+
+    def send_codes():
+        fetch_left.wait()
+        encode_rows(left_in, left_out, left.shape[1])
+        keep_left = pltpu.make_async_copy(left_out, left_code, code_sem.at[2])
+        keep_left.start()
+        fetch_right.wait()
+        encode_rows(right_in, right_out, width)
+        keep_right = pltpu.make_async_copy(right_out, right_code, code_sem.at[3])
+        keep_right.start()
+        keep_left.wait()
+        for m in range(near, 0, -1):
+            first_left(m).start()
+        own_left.start()
+        keep_right.wait()
+        each_across(0, small, ra_send, ra_recv, start)
+        each_along(0, (0,), small, rb_send, rb_recv, own_small, start, start)
+
+    def forward(k, arrays, a_s, a_r, b_s, b_r, own):
+        for ds in order:
+            for g in range(ng):
+                arrived(k, ds, g, *arrays, a_s, a_r)
+                along(k, ds, g, *arrays, b_s, b_r, own, start, start)
+
+    for k in range(FINE):
+        forward(k, fine, fa_send, fa_recv, fb_send, fb_recv, own_fine)
+    each_along(1, (0,), big, b_send, b_recv, own_big, start, start)
+
+    @pl.loop(1, CHUNKS)
     def _(k):
         @pl.when(k + AHEAD < CHUNKS)
         def _():
@@ -232,15 +318,19 @@
             for g in range(ng):
                 late_own(g).start()
 
-        forward(k)
-
-        for at, act in ((1, pass_left), (5, spread_left), (9, share_left)):
+        forward(k, big, a_send, a_recv, b_send, b_recv, own_big)
+
+        @pl.when(k + 1 < CHUNKS)
+        def _():
+            each_along(k + 1, (0,), big, b_send, b_recv, own_big, start, start)
+
+        for at, act in ((CODE_AT, send_codes), (PASS_AT, pass_left), (SPREAD_AT, spread_left), (SHARE_AT, share_left)):
             pl.when(k == at)(act)
 
-        @pl.when(k == 0)
-        def _():
-            for g in range(ng):
-                for ds in range(1, nc):
+        @pl.when(k == SMALL_AT)
+        def _():
+            for g in range(ng):
+                for ds in order:
                     arrived(0, ds, g, *small, ra_send, ra_recv)
             each_along(0, range(1, nc), small, rb_send, rb_recv, own_small, start, start)
 
@@ -263,16 +353,39 @@
         each_across(k, arrays, *a, wait_send)
         each_along(k, range(nc), arrays, b_s, b_r, own, wait_send, finish)
         for dq in range(1, nr):
-            received(k, dq, arrays[1], arrays[3], arrays[0].shape[0], b_s, b_r)
+            received(k, dq, arrays[1], arrays[3], tall(arrays[0]), b_s, b_r)
+
+    drain(0, small, (ra_send, ra_recv), rb_send, rb_recv, own_small)
+    words = pltpu.make_async_copy(right_codes, right_words, code_sem.at[0])
+    words.start()
+    words.wait()
+    decode_rows(right_words, right_values)
+    values = pltpu.make_async_copy(right_values, right_all, code_sem.at[1])
+    values.start()
+    values.wait()
+
+    @pl.loop(0, nr)
+    def _(q):
+        part = left_codes.at[:, pl.ds(pl.multiple_of(q * left_width, 128), left_width)]
+        rows = left.shape[1]
+        to = left_all.at[:, pl.ds(pl.multiple_of(q * rows, 128), rows)]
+        words = pltpu.make_async_copy(part, left_words, code_sem.at[2])
+        words.start()
+        words.wait()
+        decode_rows(left_words, left_values)
+        values = pltpu.make_async_copy(left_values, to, code_sem.at[3])
+        values.start()
+        values.wait()
 
     each_late(wait_send)
     for g in range(ng):
         late_own(g).wait()
         for ds in range(1, nc):
             late_arrived(ds, g)
-    drain(0, small, (ra_send, ra_recv), rb_send, rb_recv, own_small)
-
-    @pl.loop(0, CHUNKS)
+    for k in range(FINE):
+        drain(k, fine, (fa_send, fa_recv), fb_send, fb_recv, own_fine)
+
+    @pl.loop(1, CHUNKS)
     def _(k):
         drain(k, big, (a_send, a_recv), b_send, b_recv, own_big)
 
@@ -289,6 +402,8 @@
     main_rows = height // PARTS * CHUNKS
     late_rows = height - main_rows
     out = jax.ShapeDtypeStruct
+    code = jnp.bfloat16
+    vmem = pltpu.VMEM
     dma = pltpu.SemaphoreType.DMA
     anywhere = pl.BlockSpec(memory_space=pl.ANY)
 
@@ -304,18 +419,27 @@
             out((nr * depth, width), right_factor.dtype),
             out((nr, late_rows, width), base_weight.dtype),
             out((nc, ng, main_rows, width), base_weight.dtype),
-            out((nc, ng, depth, width), right_factor.dtype),
+            out((nc, ng, depth, width + LANES), code),
+            out((1, rank, left_width + LANES), code),
+            out((nc * rank, nr * (left_width + LANES)), code),
+            out((nr, depth, width + LANES), code),
+            out((nr * depth, width + LANES), code),
         ],
         in_specs=[anywhere] * 3,
-        out_specs=[anywhere] * 6,
+        out_specs=[anywhere] * 10,
         scratch_shapes=[
             *stage_sems(CHUNKS),
+            *stage_sems(FINE),
             *stage_sems(1),
             dma((planes - 1,)), dma((planes - 1,)),
             dma((planes, nc - 1)), dma((planes, nc - 1)),
             dma((planes, nc)), dma((planes, nc)),
             dma((nc - 1, ng)), dma((nc - 1, ng)),
-            dma((CHUNKS + 2 + ng,)),
+            dma((CHUNKS + 2 + ng + FINE,)), dma((4,)),
+            vmem((rank, left_width), jnp.float32), vmem((1, rank, left_width + LANES), code),
+            vmem((depth, stored_width), jnp.float32), vmem((nr, depth, width + LANES), code),
+            vmem((nc * rank, left_width + LANES), code), vmem((nc * rank, left_width), jnp.float32),
+            vmem((nr * depth, width + LANES), code), vmem((nr * depth, width), jnp.float32),
         ],
         compiler_params=pltpu.CompilerParams(collective_id=0, has_side_effects=True),
     )(base_weight, left_turned, right_factor)
@@ -330,7 +454,7 @@
 def body(base_weight, left_factor, right_factor):
     nr = lax.axis_size("row")
     height = base_weight.shape[0]
-    served, left_all, right_all, tail, _, _ = move(base_weight, left_factor.T, right_factor)
+    served, left_all, right_all, tail, *_ = move(base_weight, left_factor.T, right_factor)
     late = lax.all_to_all(tail, "row", 0, 0)
     late_rows, width = late.shape[1:]
     merged = (served.astype(jnp.float32) + product(left_all, right_all)).astype(jnp.bfloat16)

time: 1160 us -> 1140 us (0.983)
  Pallas kernels: 1080 us -> 1040 us
  starting transfers between devices: 3.62 us -> 17.2 us
    pallas_call x1, Pallas kernels: 1080 us -> 1040 us  [move(): pl.pallas_call(functools.partial(transport, nr, nc), out_shape=[out((nr *...]
    all_to_all x1, starting transfers between devices: 3.62 us -> 17.2 us  [body(): late = lax.all_to_all(tail, 'row', 0, 0)]
where the time goes in v3:
time: 1140 us
  Pallas kernels  1040 us (91%)
  matrix products  57.3 us (5%)
  starting transfers between devices  17.2 us (2%)
    pallas_call x1, Pallas kernels, move(): pl.pallas_call(functools.partial(transport, nr, nc), out_shape=[out((nr *...  1040 us
    dot_general x2, matrix products, product(): lax.dot_general(left, right, (((0,), (0,)), ((), ())), precision=lax.Prec...  57.3 us
  transfers between devices with their start and end apart: 1, of which 1 were waited for; matrix products, arithmetic and copies ran while one was open for 6% of the time, Pallas kernels for 0%

profile of v3, /device:TPU:5, one launch (start us, length us, event | category | flops | bytes accessed | tf_op | source)
XLA Modules:
  0.0 1137.1 jit_solution(685971870225769997)
XLA Ops:
  0.0 1043.9 %shard_map.37 = (bf16[16384,1536]{1,0:T(8,128)(2,1)}, f32[256,16384]{1,0:T(8,128)}, f32[256,1536]{1,0:T(8,128)}, bf16[8,128,1536]{2,1,0:T(8,128)(2,1)}, bf16[4,2...) custom-call(bf16[2048,12288]{1,0:T(8,128)(2,1)} %base.1, ...), custom_call_target="tpu_custom_call" | custom-call | tf_op jit(solution)/shard_map/pallas_call | solution.py:414
  1043.9 17.2 %all-to-all-start = ((bf16[8,128,1536]{2,1,0:T(8,128)(2,1)}), bf16[8,128,1536]{2,1,0:T(8,128)(2,1)S(1)}, u32[]{:S(2)}, u32[]{:S(2)}) async-start(bf16[8,128,1536]{2,1,0:T(8,128)(2,1)} %get-tuple-element.24), calls=%async_computation | async-start | bytes 6291456 | tf_op jit(solution)/shard_map/all_to_all | solution.py:458
  1061.1 0.0 copy-start
  1061.1 1.0 slice_dynamic-update-slice_fusion.7
  1062.1 0.9 slice_dynamic-update-slice_fusion.6
  1063.1 0.9 slice_dynamic-update-slice_fusion.5
  1064.0 0.9 slice_dynamic-update-slice_fusion.4
  1064.9 0.9 slice_dynamic-update-slice_fusion.3
  1065.8 0.9 slice_dynamic-update-slice_fusion.2
  1066.7 0.9 slice_dynamic-update-slice_fusion.1
  1067.7 0.9 slice_dynamic-update-slice_fusion
  1068.6 6.0 fusion.1
  1074.6 0.0 copy-done
  1074.6 51.2 %add_convert_fusion = bf16[16384,1536]{1,0:T(8,128)(2,1)} fusion(bf16[16384,1536]{1,0:T(8,128)(2,1)} %get-tuple-element.21, f32[256,16384]{1,0:T(8,128)} %get-tuple-element.22, f32[256,1536]{1,0:T(8,128)S(1)} %copy-done), kind=kOutput, calls=%fused_computation | convolution fusion | flops 38730203136 | bytes 119013376 | tf_op jit(solution)/shard_map/dot_general | solution.py:449
  1125.8 5.8 all-to-all-done
  1131.6 5.5 fusion
Async XLA Ops:
  1043.9 87.8 %all-to-all-start = ((bf16[8,128,1536]{2,1,0:T(8,128)(2,1)}), bf16[8,128,1536]{2,1,0:T(8,128)(2,1)S(1)}, u32[]{:S(2)}, u32[]{:S(2)}) async-start(bf16[8,128,1536]{2,1,0:T(8,128)(2,1)} %get-tuple-element.24), calls=%async_computation | async-start | bytes 6291456 | tf_op jit(solution)/shard_map/all_to_all | solution.py:458
  1061.1 13.5 %copy-start = (f32[256,1536]{1,0:T(8,128)S(1)}, f32[256,1536]{1,0:T(8,128)}, u32[]{:S(2)}) copy-start(f32[256,1536]{1,0:T(8,128)} %get-tuple-element.23) | copy-start | bytes 4718596

commit v4 on v3

--- a/solution.py
+++ b/solution.py
@@ -10,12 +10,14 @@
 PARTS = 16
 CHUNKS = 15
 FINE = 8
+LATE = 16
+LATE_PARTS = 1
 AHEAD = 4
-CODE_AT = 1
-PASS_AT = 3
-SMALL_AT = 6
-SPREAD_AT = 7
-SHARE_AT = 13
+CODE_AT = 5
+PASS_AT = 4
+SMALL_AT = 10
+SPREAD_AT = 10
+SHARE_AT = 14
 MESH = pl.DeviceIdType.MESH
 LANES = 128
 GROUP = 16
@@ -62,7 +64,7 @@
 
 
 def transport(
-    nr, nc, base, left, right, served, left_all, right_all, tail, mid, mid_right,
+    nr, nc, base, left, right, served, left_all, right_all, left_late, tail, mid, mid_right,
     left_code, left_codes, right_code, right_codes, *scratch,
 ):
     (a_send, a_recv, b_send, b_recv, fa_send, fa_recv, fb_send, fb_recv, ra_send, ra_recv, rb_send, rb_recv,
@@ -77,7 +79,9 @@
     rank = left.shape[0]
     left_width = left_code.shape[2]
     step = height // PARTS
-    late_rows = height - CHUNKS * step
+    late_rows = height // LATE * LATE_PARTS
+    main_rows = height - late_rows
+    over_rows = main_rows - CHUNKS * step
     r = lax.axis_index("row")
     c = lax.axis_index("col")
     sibling = r + 1 - 2 * lax.rem(r, 2)
@@ -98,16 +102,16 @@
     def tall(src):
         return src.shape[-2]
 
-    def across(k, dj, g, src, final, middle, rows, send, recv, act):
+    def across(k, dj, g, src, final, middle, rows, off, send, recv, act):
         j = shifted(c, dj, nc)
         here = c * ng + g == r
-        at = pl.ds(pl.multiple_of(k * rows, 8), rows)
+        at = pl.ds(pl.multiple_of(off + k * rows, 8), rows)
         source = piece(src, at, g * nc + j)
         sem = (k, dj - 1, g)
 
         @pl.when(here)
         def _():
-            to = final.at[pl.ds(pl.multiple_of(r * tall(src) + k * rows, 8), rows), :]
+            to = final.at[pl.ds(pl.multiple_of(r * tall(src) + off + k * rows, 8), rows), :]
             act(remote(source, to, send.at[sem], recv.at[sem], r, j))
 
         @pl.when(jnp.logical_not(here))
@@ -121,15 +125,15 @@
     def wait_send(copy):
         copy.wait_send()
 
-    def arrived(k, ds, g, src, final, middle, rows, send, recv):
-        at = pl.ds(pl.multiple_of(k * rows, 8), rows)
+    def arrived(k, ds, g, src, final, middle, rows, off, send, recv):
+        at = pl.ds(pl.multiple_of(off + k * rows, 8), rows)
         s = shifted(c, -ds, nc)
         here = s * ng + g == r
         sem = (k, ds - 1, g)
 
         @pl.when(here)
         def _():
-            to = final.at[pl.ds(pl.multiple_of(r * tall(src) + k * rows, 8), rows), :]
+            to = final.at[pl.ds(pl.multiple_of(r * tall(src) + off + k * rows, 8), rows), :]
             remote(to, to, send.at[sem], recv.at[sem], r, s).wait_recv()
 
         @pl.when(jnp.logical_not(here))
@@ -137,15 +141,15 @@
             to = middle.at[s, g, at, :]
             remote(to, to, send.at[sem], recv.at[sem], r, s).wait_recv()
 
-    def along(k, ds, g, src, final, middle, rows, send, recv, own, act, act_own):
-        at = pl.ds(pl.multiple_of(k * rows, 8), rows)
+    def along(k, ds, g, src, final, middle, rows, off, send, recv, own, act, act_own):
+        at = pl.ds(pl.multiple_of(off + k * rows, 8), rows)
         s = shifted(c, -ds, nc)
         to_row = s * ng + g
         if ds == 0:
             source = piece(src, at, g * nc + c)
         else:
             source = middle.at[s, g, at, :]
-        to = final.at[pl.ds(pl.multiple_of(r * tall(src) + k * rows, 8), rows), :]
+        to = final.at[pl.ds(pl.multiple_of(r * tall(src) + off + k * rows, 8), rows), :]
 
         @pl.when(to_row != r)
         def _():
@@ -156,14 +160,14 @@
             def _():
                 act_own(pltpu.make_async_copy(source, to, own.at[k]))
 
-    def received(k, dq, final, rows, total, send, recv):
+    def received(k, dq, final, rows, off, total, send, recv):
         q = shifted(r, -dq, nr)
-        to = final.at[pl.ds(pl.multiple_of(q * total + k * rows, 8), rows), :]
+        to = final.at[pl.ds(pl.multiple_of(q * total + off + k * rows, 8), rows), :]
         remote(to, to, send.at[k, 0, 0], recv.at[k, q], q, c).wait_recv()
 
-    big = (base, served, mid, step)
-    fine = (base, served, mid, step // FINE)
-    small = (right_code, right_codes, mid_right, depth)
+    big = (base, served, mid, step, over_rows)
+    fine = (base, served, mid, (step + over_rows) // FINE, 0)
+    small = (right_code, right_codes, mid_right, depth, 0)
     order = (nc // 2, *(d for d in range(1, nc) if d != nc // 2))
     own_big = own_sem.at[pl.ds(0, CHUNKS)]
     own_small = own_sem.at[pl.ds(CHUNKS, 1)]
@@ -181,7 +185,7 @@
 
     def late_across(dj, g, act):
         j = shifted(c, dj, nc)
-        source = base.at[pl.ds(CHUNKS * step, late_rows), pl.ds(pl.multiple_of((g * nc + j) * width, 128), width)]
+        source = base.at[pl.ds(main_rows, late_rows), pl.ds(pl.multiple_of((g * nc + j) * width, 128), width)]
         act(remote(source, tail.at[c * ng + g], t_send.at[dj - 1, g], t_recv.at[dj - 1, g], r, j))
 
     def late_arrived(ds, g):
@@ -190,7 +194,7 @@
         remote(to, to, t_send.at[ds - 1, g], t_recv.at[ds - 1, g], r, s).wait_recv()
 
     def late_own(g):
-        source = base.at[pl.ds(CHUNKS * step, late_rows), pl.ds(pl.multiple_of((g * nc + c) * width, 128), width)]
+        source = base.at[pl.ds(main_rows, late_rows), pl.ds(pl.multiple_of((g * nc + c) * width, 128), width)]
         return pltpu.make_async_copy(source, tail.at[c * ng + g], own_sem.at[CHUNKS + 2 + g])
 
     def each_late(act):
@@ -279,19 +283,21 @@
 
     own_left = pltpu.make_async_copy(left_code.at[0], block(c, r), own_sem.at[CHUNKS + 1])
 
-    def send_codes():
+    def send_left():
         fetch_left.wait()
         encode_rows(left_in, left_out, left.shape[1])
         keep_left = pltpu.make_async_copy(left_out, left_code, code_sem.at[2])
         keep_left.start()
+        keep_left.wait()
+        for m in range(near, 0, -1):
+            first_left(m).start()
+        own_left.start()
+
+    def send_right():
         fetch_right.wait()
         encode_rows(right_in, right_out, width)
         keep_right = pltpu.make_async_copy(right_out, right_code, code_sem.at[3])
         keep_right.start()
-        keep_left.wait()
-        for m in range(near, 0, -1):
-            first_left(m).start()
-        own_left.start()
         keep_right.wait()
         each_across(0, small, ra_send, ra_recv, start)
         each_along(0, (0,), small, rb_send, rb_recv, own_small, start, start)
@@ -302,6 +308,7 @@
                 arrived(k, ds, g, *arrays, a_s, a_r)
                 along(k, ds, g, *arrays, b_s, b_r, own, start, start)
 
+    send_left()
     for k in range(FINE):
         forward(k, fine, fa_send, fa_recv, fb_send, fb_recv, own_fine)
     each_along(1, (0,), big, b_send, b_recv, own_big, start, start)
@@ -324,7 +331,7 @@
         def _():
             each_along(k + 1, (0,), big, b_send, b_recv, own_big, start, start)
 
-        for at, act in ((CODE_AT, send_codes), (PASS_AT, pass_left), (SPREAD_AT, spread_left), (SHARE_AT, share_left)):
+        for at, act in ((CODE_AT, send_right), (PASS_AT, pass_left), (SPREAD_AT, spread_left), (SHARE_AT, share_left)):
             pl.when(k == at)(act)
 
         @pl.when(k == SMALL_AT)
@@ -353,7 +360,7 @@
         each_across(k, arrays, *a, wait_send)
         each_along(k, range(nc), arrays, b_s, b_r, own, wait_send, finish)
         for dq in range(1, nr):
-            received(k, dq, arrays[1], arrays[3], tall(arrays[0]), b_s, b_r)
+            received(k, dq, arrays[1], arrays[3], arrays[4], tall(arrays[0]), b_s, b_r)
 
     drain(0, small, (ra_send, ra_recv), rb_send, rb_recv, own_small)
     words = pltpu.make_async_copy(right_codes, right_words, code_sem.at[0])
@@ -375,7 +382,11 @@
         decode_rows(left_words, left_values)
         values = pltpu.make_async_copy(left_values, to, code_sem.at[3])
         values.start()
+        late_to = left_late.at[:, pl.ds(pl.multiple_of(q * LANES, 128), LANES)]
+        late = pltpu.make_async_copy(left_values.at[:, pl.ds(rows - LANES, LANES)], late_to, code_sem.at[2])
+        late.start()
         values.wait()
+        late.wait()
 
     each_late(wait_send)
     for g in range(ng):
@@ -399,8 +410,8 @@
     width = stored_width // nr
     depth = right_factor.shape[0]
     rank, left_width = left_turned.shape
-    main_rows = height // PARTS * CHUNKS
-    late_rows = height - main_rows
+    late_rows = height // LATE * LATE_PARTS
+    main_rows = height - late_rows
     out = jax.ShapeDtypeStruct
     code = jnp.bfloat16
     vmem = pltpu.VMEM
@@ -417,6 +428,7 @@
             out((nr * height, width), base_weight.dtype),
             out((nc * rank, nr * left_width), left_turned.dtype),
             out((nr * depth, width), right_factor.dtype),
+            out((nc * rank, nr * LANES), left_turned.dtype),
             out((nr, late_rows, width), base_weight.dtype),
             out((nc, ng, main_rows, width), base_weight.dtype),
             out((nc, ng, depth, width + LANES), code),
@@ -426,7 +438,7 @@
             out((nr * depth, width + LANES), code),
         ],
         in_specs=[anywhere] * 3,
-        out_specs=[anywhere] * 10,
+        out_specs=[anywhere] * 11,
         scratch_shapes=[
             *stage_sems(CHUNKS),
             *stage_sems(FINE),
@@ -454,13 +466,14 @@
 def body(base_weight, left_factor, right_factor):
     nr = lax.axis_size("row")
     height = base_weight.shape[0]
-    served, left_all, right_all, tail, *_ = move(base_weight, left_factor.T, right_factor)
+    served, left_all, right_all, left_late, tail, *_ = move(base_weight, left_factor.T, right_factor)
     late = lax.all_to_all(tail, "row", 0, 0)
     late_rows, width = late.shape[1:]
+    late_delta = product(left_late, right_all).reshape(nr, -1, width)
+    late_delta = lax.optimization_barrier(late_delta[:, late_delta.shape[1] - late_rows:])
     merged = (served.astype(jnp.float32) + product(left_all, right_all)).astype(jnp.bfloat16)
-    late_left = jnp.concatenate([left_all[:, (q + 1) * height - late_rows:(q + 1) * height] for q in range(nr)], axis=1)
-    late_merged = late.astype(jnp.float32) + product(late_left, right_all).reshape(late.shape)
-    merged = merged.reshape(nr, height, width).at[:, height - late_rows:].set(late_merged.astype(jnp.bfloat16))
+    late_merged = (late.astype(jnp.float32) + late_delta).astype(jnp.bfloat16)
+    merged = merged.reshape(nr, height, width).at[:, height - late_rows:].set(late_merged)
     return merged.reshape(nr * height, width)
 
 

time: 1140 us -> 1140 us (level)
  transfers between devices with their start and end apart: 1 -> 1, of which waited for: 1 -> 1; matrix products, arithmetic and copies ran while one was open for 6% -> 5% of each run, Pallas kernels for 0% -> 0%
where the time goes in v4:
time: 1140 us
  Pallas kernels  1040 us (91%)
  matrix products  58.3 us (5%)
  starting transfers between devices  18.2 us (2%)
  waiting for transfers between devices  12.2 us (1%)
    pallas_call x1, Pallas kernels, move(): pl.pallas_call(functools.partial(transport, nr, nc), out_shape=[out((nr *...  1040 us
    dot_general x2, matrix products, product(): lax.dot_general(left, right, (((0,), (0,)), ((), ())), precision=lax.Prec...  58.3 us
  transfers between devices with their start and end apart: 1, of which 1 were waited for; matrix products, arithmetic and copies ran while one was open for 5% of the time, Pallas kernels for 0%

profile of v4, /device:TPU:5, one launch (start us, length us, event | category | flops | bytes accessed | tf_op | source)
XLA Modules:
  0.0 1135.3 jit_solution(9153310381129694612)
XLA Ops:
  0.0 1041.1 %shard_map.37 = (bf16[16384,1536]{1,0:T(8,128)(2,1)}, f32[256,16384]{1,0:T(8,128)}, f32[256,1536]{1,0:T(8,128)}, f32[256,1024]{1,0:T(8,128)}, bf16[8,128,1536]{2...) custom-call(bf16[2048,12288]{1,0:T(8,128)(2,1)} %base.1, ...), custom_call_target="tpu_custom_call" | custom-call | tf_op jit(solution)/shard_map/pallas_call | solution.py:425
  1041.1 18.2 %all-to-all-start = ((bf16[8,128,1536]{2,1,0:T(8,128)(2,1)}), bf16[8,128,1536]{2,1,0:T(8,128)(2,1)S(1)}, u32[]{:S(2)}, u32[]{:S(2)}) async-start(bf16[8,128,1536]{2,1,0:T(8,128)(2,1)} %get-tuple-element.25), calls=%async_computation | async-start | bytes 6291456 | tf_op jit(solution)/shard_map/all_to_all | solution.py:470
  1059.3 0.0 copy-start
  1059.3 7.1 fusion.1
  1066.4 0.0 copy-done
  1066.4 51.2 %add_convert_fusion = bf16[16384,1536]{1,0:T(8,128)(2,1)} fusion(bf16[16384,1536]{1,0:T(8,128)(2,1)} %get-tuple-element.22, f32[256,16384]{1,0:T(8,128)} %get-tuple-element.23, f32[256,1536]{1,0:T(8,128)S(1)} %copy-done), kind=kOutput, calls=%fused_computation | convolution fusion | flops 38730203136 | bytes 119013376 | tf_op jit(solution)/shard_map/dot_general | solution.py:461
  1117.6 12.2 %all-to-all-done = bf16[8,128,1536]{2,1,0:T(8,128)(2,1)S(1)} async-done(((bf16[8,128,1536]{2,1,0:T(8,128)(2,1)}), bf16[8,128,1536]{2,1,0:T(8,128)(2,1)S(1)}, u32[]{:S(2)}, u32[]{:S(2)}) %all-to-all-start) | async-done | bytes 3145760 | tf_op jit(solution)/shard_map/all_to_all | solution.py:470
  1129.8 5.5 fusion
Async XLA Ops:
  1041.1 88.8 %all-to-all-start = ((bf16[8,128,1536]{2,1,0:T(8,128)(2,1)}), bf16[8,128,1536]{2,1,0:T(8,128)(2,1)S(1)}, u32[]{:S(2)}, u32[]{:S(2)}) async-start(bf16[8,128,1536]{2,1,0:T(8,128)(2,1)} %get-tuple-element.25), calls=%async_computation | async-start | bytes 6291456 | tf_op jit(solution)/shard_map/all_to_all | solution.py:470
  1059.3 7.1 copy-start

commit v5 on v4

--- a/solution.py
+++ b/solution.py
@@ -7,17 +7,16 @@
 from jax.experimental.pallas import tpu as pltpu
 from jax.sharding import PartitionSpec as P
 
-PARTS = 16
-CHUNKS = 15
-FINE = 8
+CHUNKS = 10
+FINE = 6
 LATE = 16
 LATE_PARTS = 1
-AHEAD = 4
-CODE_AT = 5
-PASS_AT = 4
-SMALL_AT = 10
-SPREAD_AT = 10
-SHARE_AT = 14
+AHEAD = 3
+CODE_AT = 3
+PASS_AT = 3
+SMALL_AT = 6
+SPREAD_AT = 6
+SHARE_AT = 9
 MESH = pl.DeviceIdType.MESH
 LANES = 128
 GROUP = 16
@@ -78,9 +77,9 @@
     depth = right.shape[0]
     rank = left.shape[0]
     left_width = left_code.shape[2]
-    step = height // PARTS
     late_rows = height // LATE * LATE_PARTS
     main_rows = height - late_rows
+    step = main_rows // CHUNKS
     over_rows = main_rows - CHUNKS * step
     r = lax.axis_index("row")
     c = lax.axis_index("col")

time: 1140 us -> 1140 us (level)
  no operation moved by 1% of the time
where the time goes in v5:
time: 1140 us; the launch traced here: 1130 us
  Pallas kernels  1030 us (90%)
  matrix products  58.3 us (5%)
  starting transfers between devices  26.2 us (2%)
  waiting for transfers between devices  12.2 us (1%)
    pallas_call x1, Pallas kernels, move(): pl.pallas_call(functools.partial(transport, nr, nc), out_shape=[out((nr *...  1030 us
    dot_general x2, matrix products, product(): lax.dot_general(left, right, (((0,), (0,)), ((), ())), precision=lax.Prec...  58.3 us
    all_to_all x1, starting transfers between devices, body(): late = lax.all_to_all(tail, 'row', 0, 0)  26.2 us
  transfers between devices with their start and end apart: 1, of which 1 were waited for; matrix products, arithmetic and copies ran while one was open for 5% of the time, Pallas kernels for 0%

profile of v5, /device:TPU:5, one launch (start us, length us, event | category | flops | bytes accessed | tf_op | source)
XLA Modules:
  0.0 1133.0 jit_solution(14254164210786867476)
XLA Ops:
  0.0 1030.8 %shard_map.37 = (bf16[16384,1536]{1,0:T(8,128)(2,1)}, f32[256,16384]{1,0:T(8,128)}, f32[256,1536]{1,0:T(8,128)}, f32[256,1024]{1,0:T(8,128)}, bf16[8,128,1536]{2...) custom-call(bf16[2048,12288]{1,0:T(8,128)(2,1)} %base.1, ...), custom_call_target="tpu_custom_call" | custom-call | tf_op jit(solution)/shard_map/pallas_call | solution.py:424
  1030.8 26.2 %all-to-all-start = ((bf16[8,128,1536]{2,1,0:T(8,128)(2,1)}), bf16[8,128,1536]{2,1,0:T(8,128)(2,1)S(1)}, u32[]{:S(2)}, u32[]{:S(2)}) async-start(bf16[8,128,1536]{2,1,0:T(8,128)(2,1)} %get-tuple-element.25), calls=%async_computation | async-start | bytes 6291456 | tf_op jit(solution)/shard_map/all_to_all | solution.py:469
  1057.0 0.0 copy-start
  1057.0 7.1 fusion.1
  1064.1 0.0 copy-done
  1064.1 51.2 %add_convert_fusion = bf16[16384,1536]{1,0:T(8,128)(2,1)} fusion(bf16[16384,1536]{1,0:T(8,128)(2,1)} %get-tuple-element.22, f32[256,16384]{1,0:T(8,128)} %get-tuple-element.23, f32[256,1536]{1,0:T(8,128)S(1)} %copy-done), kind=kOutput, calls=%fused_computation | convolution fusion | flops 38730203136 | bytes 119013376 | tf_op jit(solution)/shard_map/dot_general | solution.py:460
  1115.3 12.2 %all-to-all-done = bf16[8,128,1536]{2,1,0:T(8,128)(2,1)S(1)} async-done(((bf16[8,128,1536]{2,1,0:T(8,128)(2,1)}), bf16[8,128,1536]{2,1,0:T(8,128)(2,1)S(1)}, u32[]{:S(2)}, u32[]{:S(2)}) %all-to-all-start) | async-done | bytes 3145760 | tf_op jit(solution)/shard_map/all_to_all | solution.py:469
  1127.5 5.5 fusion
Async XLA Ops:
  1030.8 96.8 %all-to-all-start = ((bf16[8,128,1536]{2,1,0:T(8,128)(2,1)}), bf16[8,128,1536]{2,1,0:T(8,128)(2,1)S(1)}, u32[]{:S(2)}, u32[]{:S(2)}) async-start(bf16[8,128,1536]{2,1,0:T(8,128)(2,1)} %get-tuple-element.25), calls=%async_computation | async-start | bytes 6291456 | tf_op jit(solution)/shard_map/all_to_all | solution.py:469
  1057.0 7.1 copy-start
